TPU v7x, 128 devices: a whole 4x4x4 slice. The times are simulated.
128 devices in a mesh: dp: 16 (over z, x_lo, core), space: 8 (over x_hi, y).
Axes of the slice: x: 4 (x_hi: 2, x_lo: 2; x = x_hi * 2 + x_lo), y: 4, z: 4, core: 2. Of those that a mesh axis runs over, the one named last changes fastest.
Arguments:
- features: bfloat16 [16, 128, 64, 1024], P('dp', 'space'), may hold values from -6 to 6
- target: bfloat16 [16, 128, 64, 1024], P('dp', 'space'), may hold values from -6 to 6
- anchors: int32 [16, 2], P('dp'), may hold values from 0 to 64512
- w_first: bfloat16 [3, 3, 64, 64], replicated, may hold values from -0.25 to 0.25
- b_first: float32 [64], replicated, may hold values from -3 to 3
- w_second: bfloat16 [3, 3, 64, 64], replicated, may hold values from -0.25 to 0.25
- b_second: float32 [64], replicated, may hold values from -3 to 3
Outputs:
- back_input: bfloat16 [16, 128, 64, 1024], P('dp', 'space')
- grad_w1: float32 [3, 3, 64, 64], replicated
- grad_b1: float32 [64], replicated
- grad_w2: float32 [3, 3, 64, 64], replicated
- grad_b2: float32 [64], replicated
All inputs are finite; a program needn't handle non-finite values.
Results may differ from a plain program's by a relative error of at most 0.0075.
Values may be sent and summed in bfloat16 or wider, within the bound.
No kernel may reach another device: no remote copies, remote signals or barrier semaphores. Data moves between devices by JAX's collectives and lax.ppermute only.
A program may use at most 128 MiB of HBM per device.

v0:
```python
import math
import jax
import jax.numpy as jnp
from jax import lax
from jax.sharding import PartitionSpec as P


def extended(value, sides, width):
    for axis, dim in sides:
        size, length = (lax.axis_size(axis), value.shape[dim])
        up = [(i, (i + 1) % size) for i in range(size - 1)]
        down = [(j, i) for i, j in up]
        last = lax.slice_in_dim(value, length - width, length, axis=dim)
        first = lax.slice_in_dim(value, 0, width, axis=dim)
        before = lax.ppermute(last, axis, up)
        after = lax.ppermute(first, axis, down)
        value = jnp.concatenate([before, value, after], axis=dim)
    return value


def shift_cols(tensor, offset):
    if offset == 0:
        return tensor
    filler = jnp.zeros(tensor.shape[:-1] + (1,), tensor.dtype)
    if offset > 0:
        return jnp.concatenate([tensor[..., 1:], filler], axis=-1)
    return jnp.concatenate([filler, tensor[..., :-1]], axis=-1)


def unfold(padded):
    inner = padded.shape[1] - 2
    pieces = [
        shift_cols(padded[:, row_off : row_off + inner], col_off - 1)
        for row_off in range(3)
        for col_off in range(3)
    ]
    return jnp.concatenate(pieces, axis=2)


def unfold_back(padded):
    inner = padded.shape[1] - 2
    pieces = [
        shift_cols(padded[:, 2 - row_off : 2 - row_off + inner], 1 - col_off)
        for row_off in range(3)
        for col_off in range(3)
    ]
    return jnp.concatenate(pieces, axis=2)


def forward_matrix(kernel):
    return jnp.transpose(kernel, (2, 0, 1, 3)).reshape(kernel.shape[2], -1)


def backward_matrix(kernel):
    return jnp.transpose(kernel, (3, 0, 1, 2)).reshape(kernel.shape[3], -1)


def fold_kernel(matrix):
    channels = matrix.shape[0]
    return jnp.transpose(matrix.reshape(channels, 3, 3, -1), (1, 2, 0, 3))


def coords(anchor_rows, row_ids, columns, channels):
    chan_ids = jnp.arange(channels, dtype=jnp.int32)
    periods = 4 * jnp.left_shift(jnp.ones_like(chan_ids), chan_ids % 8)
    scaled = 2.0 * math.pi / periods.astype(jnp.float32)
    row_pos = anchor_rows[:, 0][:, None, None] + row_ids[None, :, None]
    row_wave = jnp.sin(
        (row_pos % periods[None, None, :]).astype(jnp.float32) * scaled[None, None, :]
    )
    col_ids = jnp.arange(columns, dtype=jnp.int32)
    col_pos = anchor_rows[:, 1][:, None, None] + col_ids[None, None, :]
    col_wave = jnp.sin(
        (col_pos % periods[None, :, None]).astype(jnp.float32) * scaled[None, :, None]
    )
    use_rows = (chan_ids < channels // 2)[None, None, :, None]
    return jnp.where(use_rows, row_wave[..., None], col_wave[:, None])


def gelu_grad(pre_act, upstream):
    return jax.vjp(lambda inputs: jax.nn.gelu(inputs, approximate=True), pre_act)[1](upstream)[0]


def mixing(form, left, right):
    return jnp.einsum(form, left, right, preferred_element_type=jnp.float32)


def combine(pairs):
    flat_grads = jnp.concatenate([piece.reshape(-1) for pair in pairs for piece in pair])
    total = lax.psum(flat_grads, ("dp", "space"))
    results = []
    start = 0
    for pair in pairs:
        for piece in pair:
            count = piece.size
            results.append(total[start : start + count].reshape(piece.shape))
            start = start + count
    return results


def shards(features, target, anchors, w_first, b_first, w_second, b_second):
    strip_rows = features.shape[1]
    columns = features.shape[3]
    channels = features.shape[2]
    dev_index = lax.axis_index("space")
    crop_rows = strip_rows * lax.axis_size("space")
    factor = 1.0 / math.sqrt(features.shape[0] * lax.axis_size("dp") * crop_rows * columns)
    row_ids = dev_index * strip_rows + jnp.arange(strip_rows, dtype=jnp.int32)
    geo = coords(anchors, row_ids, columns, channels)
    first = (features.astype(jnp.float32) + geo).astype(jnp.bfloat16)
    bias_one = b_first[None, None, :, None]
    first_pad = extended(first, (("space", 1),), 1)
    pre_act = mixing("dk,brkw->brdw", forward_matrix(w_first), unfold(first_pad)) + bias_one
    hidden = jax.nn.gelu(pre_act, approximate=True).astype(jnp.bfloat16)
    hidden_pad = extended(hidden, (("space", 1),), 1)
    output = (
        mixing("dk,brkw->brdw", forward_matrix(w_second), unfold(hidden_pad))
        + b_second[None, None, :, None]
    )
    misfit = (output - target.astype(jnp.float32)).astype(jnp.bfloat16)
    grad_w2 = fold_kernel(mixing("brdw,brkw->dk", misfit, unfold(hidden_pad))) * factor
    grad_b2 = jnp.sum(misfit.astype(jnp.float32), axis=(0, 1, 3)) * factor
    misfit_pad = extended(misfit, (("space", 1),), 1)
    back_hidden = mixing("ck,brkw->brcw", backward_matrix(w_second), unfold_back(misfit_pad))
    slope = gelu_grad(pre_act, back_hidden).astype(jnp.bfloat16)
    grad_w1 = fold_kernel(mixing("brdw,brkw->dk", slope, unfold(first_pad))) * factor
    grad_b1 = jnp.sum(slope.astype(jnp.float32), axis=(0, 1, 3)) * factor
    slope_pad = extended(slope, (("space", 1),), 1)
    back_input = mixing("ck,brkw->brcw", backward_matrix(w_first), unfold_back(slope_pad)).astype(
        jnp.bfloat16
    )
    grad_w2, grad_b2, grad_w1, grad_b1 = combine([(grad_w2, grad_b2), (grad_w1, grad_b1)])
    return (back_input, grad_w1, grad_b1, grad_w2, grad_b2)


def solution(mesh):
    in_specs = (
        P("dp", "space", None, None),
        P("dp", "space", None, None),
        P("dp", None),
        P(),
        P(),
        P(),
        P(),
    )
    out_specs = (P("dp", "space", None, None), P(), P(), P(), P())
    return jax.shard_map(shards, mesh=mesh, in_specs=in_specs, out_specs=out_specs, check_vma=False)
```

profile of v0, /device:TPU:1, one launch (start us, length us, event | category | flops | bytes accessed | tf_op | source)
XLA Modules:
  0.0 301.8 jit_solution(5083959459954517360)
XLA Ops:
  7.3 1.3 fusion.122
  10.2 3.5 %fusion.106 = f32[64,1024]{1,0:T(8,128)S(1)} fusion(f32[64]{0:T(128)S(1)} %convert_divide_fusion, s32[64]{0:T(128)S(1)} %compare_select_fusion, s32[1024]{0:T(1024)S(1)} %iota_add_fusion, pred[64]{0:T(512)(128)(4,1)S(1)} %broadcast_compare_fusion), kind=kLoop, calls=%fused_computation.138 | loop fusion | flops 589824 | bytes 266816 | tf_op jit(solution)/shard_map/sin | solution.py:73
  13.6 2.1 add_convert_fusion
  15.8 1.3 collective-permute-start.1
  17.1 4.8 %collective-permute-start = (bf16[1,1,64,1024]{3,2,1,0:T(8,128)(2,1)S(1)}, bf16[1,1,64,1024]{3,2,1,0:T(8,128)(2,1)S(1)}, u32[]{:S(2)}, u32[]{:S(2)}) collective-permute-start(bf16[1,1,64,1024]{3,2,1,0:T(8,128)(2,1)S(1)} %get-tuple-element.28), channel_id=1, source_target_pairs={{0,1},{1,2},{2,3},{3,4},{4,5},{5,6},{6,7},{8,9},{9,10},{10,11},{11... | collective-permute-start | bytes 393224 | tf_op jit(solution)/shard_map/ppermute | solution.py:15
  31.6 8.4 %fusion.35 = (bf16[1,16,64,1024]{3,2,1,0:T(8,128)(2,1)S(1)}, f32[16,1024,64]{1,2,0:T(8,128)}) fusion(f32[64]{0:T(128)S(1)} %copy-done.6, bf16[64,576,1]{0,1,2:T(8,128)(2,1)S(1)} %bitcast.173, bf16[1,16,576,1024]{3,2,1,0:T(8,128)(2,1)S(1)} %fusion.65), kind=kOutput, calls=%fused_computation.44 | convolution fusion | flops 1218445312 | bytes 25239808 | tf_op jit(solution)/shard_map/dk,brkw->brdw/dot_general | solution.py:85
  40.0 1.3 collective-permute-start.3
  41.3 4.6 %collective-permute-start.2 = (bf16[1,1,64,1024]{3,2,1,0:T(8,128)(2,1)S(1)}, bf16[1,1,64,1024]{3,2,1,0:T(8,128)(2,1)S(1)}, u32[]{:S(2)}, u32[]{:S(2)}) collective-permute-start(bf16[1,1,64,1024]{3,2,1,0:T(8,128)(2,1)S(1)} %get-tuple-element.22), channel_id=1, source_target_pairs={{0,1},{1,2},{2,3},{3,4},{4,5},{5,6},{6,7},{8,9},{9,10},{10,11},{11... | collective-permute-start | bytes 393224 | tf_op jit(solution)/shard_map/ppermute | solution.py:15
  46.1 1.5 collective-permute-done.2
  55.1 8.4 %convert_reduce_fusion.1 = (f32[64]{0:T(128)S(1)}, bf16[1,16,64,1024]{3,2,1,0:T(8,128)(2,1)S(1)}) fusion(bf16[1,16,64,1024]{3,2,1,0:T(8,128)(2,1)} %param.8, f32[64]{0:T(128)S(1)} %copy-done.5, bf16[64,576,1]{0,1,2:T(8,128)(2,1)S(1)} %bitcast.167, bf16[1,16,576,1024]{3,2,1,0:T(8,128)(2,1)S(1)} %fusion.69), kind=kOutput, calls=%fused_computation.47 | convolution fusion | flops 1214251008 | bytes 23142912 | tf_op jit(solution)/shard_map/dk,brkw->brdw/dot_general | solution.py:85
  63.5 12.3 %fusion.92 = f32[3,3,64,64]{3,2,1,0:T(8,128)S(1)} fusion(bf16[3,3,64,16,1024]{4,2,1,0,3:T(8,128)(2,1)} %bitcast.166, bf16[1,16,64,1024]{3,2,1,0:T(8,128)(2,1)S(1)} %get-tuple-element.38), kind=kOutput, calls=%fused_computation.128 | convolution fusion | flops 1207996416 | bytes 21118976 | tf_op jit(solution)/shard_map/brdw,brkw->dk/dot_general | solution.py:85
  76.0 4.1 %collective-permute-start.5 = (bf16[1,1,64,1024]{3,2,1,0:T(8,128)(2,1)S(1)}, bf16[1,1,64,1024]{3,2,1,0:T(8,128)(2,1)S(1)}, u32[]{:S(2)}, u32[]{:S(2)}) collective-permute-start(bf16[1,1,64,1024]{3,2,1,0:T(8,128)(2,1)S(1)} %get-tuple-element.15), channel_id=1, source_target_pairs={{0,1},{1,2},{2,3},{3,4},{4,5},{5,6},{6,7},{8,9},{9,10},{10,11},{11... | collective-permute-start | bytes 393224 | tf_op jit(solution)/shard_map/ppermute | solution.py:15
  80.0 1.7 collective-permute-start.4
  82.0 5.7 %collective-permute-done.4 = bf16[1,1,64,1024]{3,2,1,0:T(8,128)(2,1)S(1)} collective-permute-done((bf16[1,1,64,1024]{3,2,1,0:T(8,128)(2,1)S(1)}, bf16[1,1,64,1024]{3,2,1,0:T(8,128)(2,1)S(1)}, u32[]{:S(2)}, u32[]{:S(2)}) %collective-permute-start.4) | collective-permute-done | bytes 131104 | tf_op jit(solution)/shard_map/ppermute | solution.py:16
  87.6 2.4 fusion.46
  95.5 10.1 %convert_reduce_fusion = (f32[64]{0:T(128)S(1)}, bf16[1,16,64,1024]{3,2,1,0:T(8,128)(2,1)S(1)}) fusion(f32[64]{0:T(128)S(1)} %copy-done.6, f32[16,1024,64]{1,2,0:T(8,128)} %get-tuple-element.36, bf16[64,576,1]{0,1,2:T(8,128)(2,1)S(1)} %bitcast.172, bf16[1,16,576,1024]{3,2,1,0:T(8,128)(2,1)S(1)} %fusion.73), kind=kOutput, calls=%fused_computation.46 | convolution fusion | flops 1232076800 | bytes 25240064 | tf_op jit(solution)/shard_map/ck,brkw->brcw/dot_general | solution.py:85
  105.6 12.5 %fusion.101 = f32[3,3,64,64]{3,2,1,0:T(8,128)S(1)} fusion(bf16[3,3,64,16,1024]{4,2,1,0,3:T(8,128)(2,1)} %bitcast.170, bf16[1,16,64,1024]{3,2,1,0:T(8,128)(2,1)S(1)} %get-tuple-element.40), kind=kOutput, calls=%fused_computation.131 | convolution fusion | flops 1207996416 | bytes 21118976 | tf_op jit(solution)/shard_map/brdw,brkw->dk/dot_general | solution.py:85
  118.3 7.4 %collective-permute-start.7 = (bf16[1,1,64,1024]{3,2,1,0:T(8,128)(2,1)S(1)}, bf16[1,1,64,1024]{3,2,1,0:T(8,128)(2,1)S(1)}, u32[]{:S(2)}, u32[]{:S(2)}) collective-permute-start(bf16[1,1,64,1024]{3,2,1,0:T(8,128)(2,1)S(1)} %get-tuple-element.9), channel_id=1, source_target_pairs={{0,1},{1,2},{2,3},{3,4},{4,5},{5,6},{6,7},{8,9},{9,10},{10,11},{11... | collective-permute-start | bytes 393224 | tf_op jit(solution)/shard_map/ppermute | solution.py:15
  125.7 1.3 collective-permute-start.6
  127.0 4.3 %concatenate.165 = f32[73856]{0:T(1024)} concatenate(f32[36864]{0:T(1024)S(1)} %reshape.374, f32[64]{0:T(128)S(1)} %broadcast_multiply_fusion.1, f32[36864]{0:T(1024)S(1)} %reshape.376, f32[64]{0:T(128)S(1)} %broadcast_multiply_fusion), dimensions={0} | concatenate | bytes 590848 | tf_op jit(solution)/shard_map/concatenate | solution.py:89
  131.3 4.1 %collective-permute-done.6 = bf16[1,1,64,1024]{3,2,1,0:T(8,128)(2,1)S(1)} collective-permute-done((bf16[1,1,64,1024]{3,2,1,0:T(8,128)(2,1)S(1)}, bf16[1,1,64,1024]{3,2,1,0:T(8,128)(2,1)S(1)}, u32[]{:S(2)}, u32[]{:S(2)}) %collective-permute-start.6) | collective-permute-done | bytes 131104 | tf_op jit(solution)/shard_map/ppermute | solution.py:16
  135.4 2.4 fusion.40
  143.2 6.7 %convert_bitcast_fusion = bf16[1,16,64,1024]{3,2,1,0:T(8,128)(2,1)} fusion(bf16[64,576,1]{0,1,2:T(8,128)(2,1)S(1)} %bitcast.169, bf16[1,16,576,1024]{3,2,1,0:T(8,128)(2,1)S(1)} %fusion.77), kind=kOutput, calls=%fused_computation.109 | convolution fusion | flops 1209008128 | bytes 21045248 | tf_op jit(solution)/shard_map/ck,brkw->brcw/dot_general | solution.py:85
  150.0 140.8 %all-reduce.26.cloned.1.call-done = f32[73856]{0:T(1024)} async-done(((f32[73856]{0:T(1024)}), f32[73856]{0:T(1024)}) %all-reduce.26.cloned.1.call-update) | async-done | bytes 295440 | tf_op jit(solution)/shard_map/psum | solution.py:90
  (80 shorter events, 34.1 us)
Async XLA Ops:
  7.2 14.8 %copy-start.2 = (bf16[3,3,64,64]{3,2,1,0:T(8,128)(2,1)S(1)}, bf16[3,3,64,64]{3,2,1,0:T(8,128)(2,1)}, u32[]{:S(2)}) copy-start(bf16[3,3,64,64]{3,2,1,0:T(8,128)(2,1)} %param.10) | copy-start | bytes 221188
  7.2 283.6 %all-reduce.26.cloned.1.call-start = ((), (), s32[]{:S(2)}) async-start(), calls=%async_computation | async-start | bytes 598016 | tf_op jit(solution)/shard_map/psum | solution.py:90
  15.8 6.9 %collective-permute-start.1 = (bf16[1,1,64,1024]{3,2,1,0:T(8,128)(2,1)S(1)}, bf16[1,1,64,1024]{3,2,1,0:T(8,128)(2,1)S(1)}, u32[]{:S(2)}, u32[]{:S(2)}) collective-permute-start(bf16[1,1,64,1024]{3,2,1,0:T(8,128)(2,1)S(1)} %get-tuple-element.27), channel_id=1, source_target_pairs={{1,0},{2,1},{3,2},{4,3},{5,4},{6,5},{7,6},{9,8},{10,9},{11,10},{12... | collective-permute-start | bytes 393224 | tf_op jit(solution)/shard_map/ppermute | solution.py:16
  17.1 6.6 %collective-permute-start = (bf16[1,1,64,1024]{3,2,1,0:T(8,128)(2,1)S(1)}, bf16[1,1,64,1024]{3,2,1,0:T(8,128)(2,1)S(1)}, u32[]{:S(2)}, u32[]{:S(2)}) collective-permute-start(bf16[1,1,64,1024]{3,2,1,0:T(8,128)(2,1)S(1)} %get-tuple-element.28), channel_id=1, source_target_pairs={{0,1},{1,2},{2,3},{3,4},{4,5},{5,6},{6,7},{8,9},{9,10},{10,11},{11... | collective-permute-start | bytes 393224 | tf_op jit(solution)/shard_map/ppermute | solution.py:15
  25.9 2.3 copy-start.1
  30.2 1.4 copy-start.6
  31.6 8.4 %copy-start.3 = (bf16[1,16,576,1024]{3,2,1,0:T(8,128)(2,1)}, bf16[1,16,576,1024]{3,2,1,0:T(8,128)(2,1)S(1)}, u32[]{:S(2)}) copy-start(bf16[1,16,576,1024]{3,2,1,0:T(8,128)(2,1)S(1)} %fusion.65) | copy-start | bytes 56623108
  31.6 14.3 %copy-start.4 = (bf16[3,3,64,64]{3,2,1,0:T(8,128)(2,1)S(1)}, bf16[3,3,64,64]{3,2,1,0:T(8,128)(2,1)}, u32[]{:S(2)}) copy-start(bf16[3,3,64,64]{3,2,1,0:T(8,128)(2,1)} %param.12) | copy-start | bytes 221188
  40.0 6.1 %collective-permute-start.3 = (bf16[1,1,64,1024]{3,2,1,0:T(8,128)(2,1)S(1)}, bf16[1,1,64,1024]{3,2,1,0:T(8,128)(2,1)S(1)}, u32[]{:S(2)}, u32[]{:S(2)}) collective-permute-start(bf16[1,1,64,1024]{3,2,1,0:T(8,128)(2,1)S(1)} %get-tuple-element.21), channel_id=1, source_target_pairs={{1,0},{2,1},{3,2},{4,3},{5,4},{6,5},{7,6},{9,8},{10,9},{11,10},{12... | collective-permute-start | bytes 393224 | tf_op jit(solution)/shard_map/ppermute | solution.py:16
  41.3 6.3 %collective-permute-start.2 = (bf16[1,1,64,1024]{3,2,1,0:T(8,128)(2,1)S(1)}, bf16[1,1,64,1024]{3,2,1,0:T(8,128)(2,1)S(1)}, u32[]{:S(2)}, u32[]{:S(2)}) collective-permute-start(bf16[1,1,64,1024]{3,2,1,0:T(8,128)(2,1)S(1)} %get-tuple-element.22), channel_id=1, source_target_pairs={{0,1},{1,2},{2,3},{3,4},{4,5},{5,6},{6,7},{8,9},{9,10},{10,11},{11... | collective-permute-start | bytes 393224 | tf_op jit(solution)/shard_map/ppermute | solution.py:15
  53.8 1.3 copy-start.5
  55.1 8.4 %copy-start = (bf16[1,16,576,1024]{3,2,1,0:T(8,128)(2,1)}, bf16[1,16,576,1024]{3,2,1,0:T(8,128)(2,1)S(1)}, u32[]{:S(2)}) copy-start(bf16[1,16,576,1024]{3,2,1,0:T(8,128)(2,1)S(1)} %fusion.69) | copy-start | bytes 56623108
  76.0 6.0 %collective-permute-start.5 = (bf16[1,1,64,1024]{3,2,1,0:T(8,128)(2,1)S(1)}, bf16[1,1,64,1024]{3,2,1,0:T(8,128)(2,1)S(1)}, u32[]{:S(2)}, u32[]{:S(2)}) collective-permute-start(bf16[1,1,64,1024]{3,2,1,0:T(8,128)(2,1)S(1)} %get-tuple-element.15), channel_id=1, source_target_pairs={{0,1},{1,2},{2,3},{3,4},{4,5},{5,6},{6,7},{8,9},{9,10},{10,11},{11... | collective-permute-start | bytes 393224 | tf_op jit(solution)/shard_map/ppermute | solution.py:15
  80.0 7.6 %collective-permute-start.4 = (bf16[1,1,64,1024]{3,2,1,0:T(8,128)(2,1)S(1)}, bf16[1,1,64,1024]{3,2,1,0:T(8,128)(2,1)S(1)}, u32[]{:S(2)}, u32[]{:S(2)}) collective-permute-start(bf16[1,1,64,1024]{3,2,1,0:T(8,128)(2,1)S(1)} %get-tuple-element.16), channel_id=1, source_target_pairs={{1,0},{2,1},{3,2},{4,3},{5,4},{6,5},{7,6},{9,8},{10,9},{11,10},{12... | collective-permute-start | bytes 393224 | tf_op jit(solution)/shard_map/ppermute | solution.py:16
  118.3 13.1 %collective-permute-start.7 = (bf16[1,1,64,1024]{3,2,1,0:T(8,128)(2,1)S(1)}, bf16[1,1,64,1024]{3,2,1,0:T(8,128)(2,1)S(1)}, u32[]{:S(2)}, u32[]{:S(2)}) collective-permute-start(bf16[1,1,64,1024]{3,2,1,0:T(8,128)(2,1)S(1)} %get-tuple-element.9), channel_id=1, source_target_pairs={{0,1},{1,2},{2,3},{3,4},{4,5},{5,6},{6,7},{8,9},{9,10},{10,11},{11... | collective-permute-start | bytes 393224 | tf_op jit(solution)/shard_map/ppermute | solution.py:15
  125.7 9.7 %collective-permute-start.6 = (bf16[1,1,64,1024]{3,2,1,0:T(8,128)(2,1)S(1)}, bf16[1,1,64,1024]{3,2,1,0:T(8,128)(2,1)S(1)}, u32[]{:S(2)}, u32[]{:S(2)}) collective-permute-start(bf16[1,1,64,1024]{3,2,1,0:T(8,128)(2,1)S(1)} %get-tuple-element.10), channel_id=1, source_target_pairs={{1,0},{2,1},{3,2},{4,3},{5,4},{6,5},{7,6},{9,8},{10,9},{11,10},{12... | collective-permute-start | bytes 393224 | tf_op jit(solution)/shard_map/ppermute | solution.py:16
Sparse Core Ops, SparseCore 0:
  131.4 159.3 all-reduce.25
where the time goes:
time: 306 us; the launch traced here: 302 us
  waiting for transfers between devices  154 us (50%)
  matrix products  58.4 us (19%)
  starting transfers between devices  26.5 us (9%)
  other arithmetic  25.8 us (8%)
  local copies, waits for them, and re-layouts  22.4 us (7%)
  between operations  14.9 us (5%)
    psum x1, waiting for transfers between devices, combine(): total = lax.psum(flat_grads, ('dp', 'space'))  141 us
    dot_general x6, matrix products, mixing(): return jnp.einsum(form, left, right, preferred_element_type=jnp.float32)  58.4 us
    ppermute x4, starting transfers between devices, extended(): before = lax.ppermute(last, axis, up)  20.9 us
    unnamed x33, local copies, waits for them, and re-layouts  12.2 us
    ppermute x4, waiting for transfers between devices, extended(): after = lax.ppermute(first, axis, down)  10.4 us
    unnamed x13, other arithmetic  7.09 us
    concatenate x4, other arithmetic, extended(): value = jnp.concatenate([before, value, after], axis=dim)  6.78 us
  transfers between devices with their start and end apart: 9, of which 7 were waited for; matrix products, arithmetic and copies ran while one was open for 6% of the time, Pallas kernels for 0%

commit v1 on v0

--- a/solution.py
+++ b/solution.py
@@ -3,6 +3,12 @@
 import jax.numpy as jnp
 from jax import lax
 from jax.sharding import PartitionSpec as P
+
+
+def ladders_track(xx, peer_axis):
+    m_next = lax.all_gather(xx, axis_name=peer_axis)
+    far_arr = jnp.sum(m_next, axis=0)
+    return far_arr
 
 
 def extended(value, sides, width):
@@ -87,7 +93,7 @@
 
 def combine(pairs):
     flat_grads = jnp.concatenate([piece.reshape(-1) for pair in pairs for piece in pair])
-    total = lax.psum(flat_grads, ("dp", "space"))
+    total = ladders_track(flat_grads, ("dp", "space"))
     results = []
     start = 0
     for pair in pairs:

time: 306 us -> 535 us (1.75)
  waiting for transfers between devices: 154 us -> 351 us
  other arithmetic: 25.8 us -> 61.4 us
    all_gather x0 -> x1, waiting for transfers between devices: none -> 334 us  [ladders_track(): m_next = lax.all_gather(xx, axis_name=peer_axis)]
    psum x1 -> x0, waiting for transfers between devices: 141 us -> none  [combine(): total = lax.psum(flat_grads, ('dp', 'space'))]
    reduce_sum x0 -> x1, other arithmetic: none -> 35.6 us  [ladders_track(): far_arr = jnp.sum(m_next, axis=0)]
    unnamed x33 -> x34, local copies, waits for them, and re-layouts: 12.2 us -> 13 us
  transfers between devices with their start and end apart: 9 -> 9, of which waited for: 7 -> 8; matrix products, arithmetic and copies ran while one was open for 6% -> 3% of each run, Pallas kernels for 0% -> 0%
where the time goes in v1:
time: 535 us; the launch traced here: 531 us
  waiting for transfers between devices  351 us (66%)
  other arithmetic  61.4 us (11%)
  matrix products  58.4 us (11%)
  starting transfers between devices  26.5 us (5%)
  local copies, waits for them, and re-layouts  18.8 us (4%)
  between operations  14.9 us (3%)
    all_gather x1, waiting for transfers between devices, ladders_track(): m_next = lax.all_gather(xx, axis_name=peer_axis)  334 us
    dot_general x6, matrix products, mixing(): return jnp.einsum(form, left, right, preferred_element_type=jnp.float32)  58.4 us
    reduce_sum x1, other arithmetic, ladders_track(): far_arr = jnp.sum(m_next, axis=0)  35.6 us
    ppermute x4, starting transfers between devices, extended(): before = lax.ppermute(last, axis, up)  20.9 us
    ppermute x4, waiting for transfers between devices, extended(): after = lax.ppermute(first, axis, down)  14.1 us
    unnamed x34, local copies, waits for them, and re-layouts  13 us
  transfers between devices with their start and end apart: 9, of which 8 were waited for; matrix products, arithmetic and copies ran while one was open for 3% of the time, Pallas kernels for 0%

profile of v1, /device:TPU:1, one launch (start us, length us, event | category | flops | bytes accessed | tf_op | source)
XLA Modules:
  0.0 531.0 jit_solution(13210614910652338709)
XLA Ops:
  7.3 1.3 fusion.122
  10.2 3.5 fusion.106
  13.6 2.1 add_convert_fusion
  15.8 1.3 collective-permute-start.1
  17.1 4.8 collective-permute-start
  31.6 8.4 %fusion.35 = (bf16[1,16,64,1024]{3,2,1,0:T(8,128)(2,1)S(1)}, f32[16,1024,64]{1,2,0:T(8,128)}) fusion(f32[64]{0:T(128)S(1)} %copy-done.6, bf16[64,576,1]{0,1,2:T(8,128)(2,1)S(1)} %bitcast.173, bf16[1,16,576,1024]{3,2,1,0:T(8,128)(2,1)S(1)} %fusion.65), kind=kOutput, calls=%fused_computation.44 | convolution fusion | flops 1218445312 | bytes 25239808 | tf_op jit(solution)/shard_map/dk,brkw->brdw/dot_general | solution.py:91
  40.0 1.3 collective-permute-start.3
  41.3 4.6 collective-permute-start.2
  46.1 1.5 collective-permute-done.2
  55.1 8.4 %convert_reduce_fusion.1 = (f32[64]{0:T(128)S(1)}, bf16[1,16,64,1024]{3,2,1,0:T(8,128)(2,1)S(1)}) fusion(bf16[1,16,64,1024]{3,2,1,0:T(8,128)(2,1)} %param.8, f32[64]{0:T(128)S(1)} %copy-done.5, bf16[64,576,1]{0,1,2:T(8,128)(2,1)S(1)} %bitcast.167, bf16[1,16,576,1024]{3,2,1,0:T(8,128)(2,1)S(1)} %fusion.69), kind=kOutput, calls=%fused_computation.47 | convolution fusion | flops 1214251008 | bytes 23142912 | tf_op jit(solution)/shard_map/dk,brkw->brdw/dot_general | solution.py:91
  63.5 12.3 %fusion.92 = f32[3,3,64,64]{3,2,1,0:T(8,128)S(1)} fusion(bf16[3,3,64,16,1024]{4,2,1,0,3:T(8,128)(2,1)} %bitcast.166, bf16[1,16,64,1024]{3,2,1,0:T(8,128)(2,1)S(1)} %get-tuple-element.38), kind=kOutput, calls=%fused_computation.128 | convolution fusion | flops 1207996416 | bytes 21118976 | tf_op jit(solution)/shard_map/brdw,brkw->dk/dot_general | solution.py:91
  76.0 4.1 collective-permute-start.5
  80.0 1.7 collective-permute-start.4
  82.0 5.7 %collective-permute-done.4 = bf16[1,1,64,1024]{3,2,1,0:T(8,128)(2,1)S(1)} collective-permute-done((bf16[1,1,64,1024]{3,2,1,0:T(8,128)(2,1)S(1)}, bf16[1,1,64,1024]{3,2,1,0:T(8,128)(2,1)S(1)}, u32[]{:S(2)}, u32[]{:S(2)}) %collective-permute-start.4) | collective-permute-done | bytes 131104 | tf_op jit(solution)/shard_map/ppermute | solution.py:22
  87.6 2.4 fusion.46
  95.5 10.1 %convert_reduce_fusion = (f32[64]{0:T(128)S(1)}, bf16[1,16,64,1024]{3,2,1,0:T(8,128)(2,1)S(1)}) fusion(f32[64]{0:T(128)S(1)} %copy-done.6, f32[16,1024,64]{1,2,0:T(8,128)} %get-tuple-element.36, bf16[64,576,1]{0,1,2:T(8,128)(2,1)S(1)} %bitcast.172, bf16[1,16,576,1024]{3,2,1,0:T(8,128)(2,1)S(1)} %fusion.73), kind=kOutput, calls=%fused_computation.46 | convolution fusion | flops 1232076800 | bytes 25240064 | tf_op jit(solution)/shard_map/ck,brkw->brcw/dot_general | solution.py:91
  105.6 12.5 %fusion.101 = f32[3,3,64,64]{3,2,1,0:T(8,128)S(1)} fusion(bf16[3,3,64,16,1024]{4,2,1,0,3:T(8,128)(2,1)} %bitcast.170, bf16[1,16,64,1024]{3,2,1,0:T(8,128)(2,1)S(1)} %get-tuple-element.40), kind=kOutput, calls=%fused_computation.131 | convolution fusion | flops 1207996416 | bytes 21118976 | tf_op jit(solution)/shard_map/brdw,brkw->dk/dot_general | solution.py:91
  118.2 1.6 concatenate.165
  120.8 7.4 %collective-permute-start.7 = (bf16[1,1,64,1024]{3,2,1,0:T(8,128)(2,1)S(1)}, bf16[1,1,64,1024]{3,2,1,0:T(8,128)(2,1)S(1)}, u32[]{:S(2)}, u32[]{:S(2)}) collective-permute-start(bf16[1,1,64,1024]{3,2,1,0:T(8,128)(2,1)S(1)} %get-tuple-element.9), channel_id=1, source_target_pairs={{0,1},{1,2},{2,3},{3,4},{4,5},{5,6},{6,7},{8,9},{9,10},{10,11},{11... | collective-permute-start | bytes 393224 | tf_op jit(solution)/shard_map/ppermute | solution.py:21
  130.1 7.8 %collective-permute-done.6 = bf16[1,1,64,1024]{3,2,1,0:T(8,128)(2,1)S(1)} collective-permute-done((bf16[1,1,64,1024]{3,2,1,0:T(8,128)(2,1)S(1)}, bf16[1,1,64,1024]{3,2,1,0:T(8,128)(2,1)S(1)}, u32[]{:S(2)}, u32[]{:S(2)}) %collective-permute-start.6) | collective-permute-done | bytes 131104 | tf_op jit(solution)/shard_map/ppermute | solution.py:22
  137.9 2.4 fusion.40
  145.7 6.7 %convert_bitcast_fusion = bf16[1,16,64,1024]{3,2,1,0:T(8,128)(2,1)} fusion(bf16[64,576,1]{0,1,2:T(8,128)(2,1)S(1)} %bitcast.169, bf16[1,16,576,1024]{3,2,1,0:T(8,128)(2,1)S(1)} %fusion.77), kind=kOutput, calls=%fused_computation.109 | convolution fusion | flops 1209008128 | bytes 21045248 | tf_op jit(solution)/shard_map/ck,brkw->brcw/dot_general | solution.py:91
  152.5 333.6 %all-gather.4.cloned.1.call-done = f32[128,1,73856]{2,1,0:T(1,128)} async-done(((f32[1,1,73856]{2,1,0:T(1,128)}), f32[128,1,73856]{2,1,0:T(1,128)}) %all-gather.4.cloned.1.call-update) | async-done | bytes 37814288 | tf_op jit(solution)/shard_map/all_gather | solution.py:9
  486.0 35.6 %reduce_sum.29 = f32[73856]{0:T(1024)S(1)} reduce(f32[128,1,73856]{2,1,0:T(1,128)} %all-gather.4.cloned.1.call-done, f32[]{:T(128)} %constant.63.clone.1), dimensions={0,1}, to_apply=%region_2.3 | reduce | flops 9379712 | bytes 38109700 | tf_op jit(solution)/shard_map/reduce_sum | solution.py:10
  (82 shorter events, 35.2 us)
Async XLA Ops:
  7.2 14.8 %copy-start.2 = (bf16[3,3,64,64]{3,2,1,0:T(8,128)(2,1)S(1)}, bf16[3,3,64,64]{3,2,1,0:T(8,128)(2,1)}, u32[]{:S(2)}) copy-start(bf16[3,3,64,64]{3,2,1,0:T(8,128)(2,1)} %param.10) | copy-start | bytes 221188
  7.2 478.9 %all-gather.4.cloned.1.call-start = ((), (), s32[]{:S(2)}) async-start(), calls=%async_computation | async-start | bytes 38109696 | tf_op jit(solution)/shard_map/all_gather | solution.py:9
  15.8 6.9 %collective-permute-start.1 = (bf16[1,1,64,1024]{3,2,1,0:T(8,128)(2,1)S(1)}, bf16[1,1,64,1024]{3,2,1,0:T(8,128)(2,1)S(1)}, u32[]{:S(2)}, u32[]{:S(2)}) collective-permute-start(bf16[1,1,64,1024]{3,2,1,0:T(8,128)(2,1)S(1)} %get-tuple-element.27), channel_id=1, source_target_pairs={{1,0},{2,1},{3,2},{4,3},{5,4},{6,5},{7,6},{9,8},{10,9},{11,10},{12... | collective-permute-start | bytes 393224 | tf_op jit(solution)/shard_map/ppermute | solution.py:22
  17.1 6.6 %collective-permute-start = (bf16[1,1,64,1024]{3,2,1,0:T(8,128)(2,1)S(1)}, bf16[1,1,64,1024]{3,2,1,0:T(8,128)(2,1)S(1)}, u32[]{:S(2)}, u32[]{:S(2)}) collective-permute-start(bf16[1,1,64,1024]{3,2,1,0:T(8,128)(2,1)S(1)} %get-tuple-element.28), channel_id=1, source_target_pairs={{0,1},{1,2},{2,3},{3,4},{4,5},{5,6},{6,7},{8,9},{9,10},{10,11},{11... | collective-permute-start | bytes 393224 | tf_op jit(solution)/shard_map/ppermute | solution.py:21
  25.9 2.3 copy-start.1
  30.2 1.4 copy-start.6
  31.6 8.4 %copy-start.3 = (bf16[1,16,576,1024]{3,2,1,0:T(8,128)(2,1)}, bf16[1,16,576,1024]{3,2,1,0:T(8,128)(2,1)S(1)}, u32[]{:S(2)}) copy-start(bf16[1,16,576,1024]{3,2,1,0:T(8,128)(2,1)S(1)} %fusion.65) | copy-start | bytes 56623108
  31.6 14.3 %copy-start.4 = (bf16[3,3,64,64]{3,2,1,0:T(8,128)(2,1)S(1)}, bf16[3,3,64,64]{3,2,1,0:T(8,128)(2,1)}, u32[]{:S(2)}) copy-start(bf16[3,3,64,64]{3,2,1,0:T(8,128)(2,1)} %param.12) | copy-start | bytes 221188
  40.0 6.1 %collective-permute-start.3 = (bf16[1,1,64,1024]{3,2,1,0:T(8,128)(2,1)S(1)}, bf16[1,1,64,1024]{3,2,1,0:T(8,128)(2,1)S(1)}, u32[]{:S(2)}, u32[]{:S(2)}) collective-permute-start(bf16[1,1,64,1024]{3,2,1,0:T(8,128)(2,1)S(1)} %get-tuple-element.21), channel_id=1, source_target_pairs={{1,0},{2,1},{3,2},{4,3},{5,4},{6,5},{7,6},{9,8},{10,9},{11,10},{12... | collective-permute-start | bytes 393224 | tf_op jit(solution)/shard_map/ppermute | solution.py:22
  41.3 6.3 %collective-permute-start.2 = (bf16[1,1,64,1024]{3,2,1,0:T(8,128)(2,1)S(1)}, bf16[1,1,64,1024]{3,2,1,0:T(8,128)(2,1)S(1)}, u32[]{:S(2)}, u32[]{:S(2)}) collective-permute-start(bf16[1,1,64,1024]{3,2,1,0:T(8,128)(2,1)S(1)} %get-tuple-element.22), channel_id=1, source_target_pairs={{0,1},{1,2},{2,3},{3,4},{4,5},{5,6},{6,7},{8,9},{9,10},{10,11},{11... | collective-permute-start | bytes 393224 | tf_op jit(solution)/shard_map/ppermute | solution.py:21
  53.8 1.3 copy-start.5
  55.1 8.4 %copy-start = (bf16[1,16,576,1024]{3,2,1,0:T(8,128)(2,1)}, bf16[1,16,576,1024]{3,2,1,0:T(8,128)(2,1)S(1)}, u32[]{:S(2)}) copy-start(bf16[1,16,576,1024]{3,2,1,0:T(8,128)(2,1)S(1)} %fusion.69) | copy-start | bytes 56623108
  76.0 6.0 %collective-permute-start.5 = (bf16[1,1,64,1024]{3,2,1,0:T(8,128)(2,1)S(1)}, bf16[1,1,64,1024]{3,2,1,0:T(8,128)(2,1)S(1)}, u32[]{:S(2)}, u32[]{:S(2)}) collective-permute-start(bf16[1,1,64,1024]{3,2,1,0:T(8,128)(2,1)S(1)} %get-tuple-element.15), channel_id=1, source_target_pairs={{0,1},{1,2},{2,3},{3,4},{4,5},{5,6},{6,7},{8,9},{9,10},{10,11},{11... | collective-permute-start | bytes 393224 | tf_op jit(solution)/shard_map/ppermute | solution.py:21
  80.0 7.6 %collective-permute-start.4 = (bf16[1,1,64,1024]{3,2,1,0:T(8,128)(2,1)S(1)}, bf16[1,1,64,1024]{3,2,1,0:T(8,128)(2,1)S(1)}, u32[]{:S(2)}, u32[]{:S(2)}) collective-permute-start(bf16[1,1,64,1024]{3,2,1,0:T(8,128)(2,1)S(1)} %get-tuple-element.16), channel_id=1, source_target_pairs={{1,0},{2,1},{3,2},{4,3},{5,4},{6,5},{7,6},{9,8},{10,9},{11,10},{12... | collective-permute-start | bytes 393224 | tf_op jit(solution)/shard_map/ppermute | solution.py:22
  120.8 9.3 %collective-permute-start.7 = (bf16[1,1,64,1024]{3,2,1,0:T(8,128)(2,1)S(1)}, bf16[1,1,64,1024]{3,2,1,0:T(8,128)(2,1)S(1)}, u32[]{:S(2)}, u32[]{:S(2)}) collective-permute-start(bf16[1,1,64,1024]{3,2,1,0:T(8,128)(2,1)S(1)} %get-tuple-element.9), channel_id=1, source_target_pairs={{0,1},{1,2},{2,3},{3,4},{4,5},{5,6},{6,7},{8,9},{9,10},{10,11},{11... | collective-permute-start | bytes 393224 | tf_op jit(solution)/shard_map/ppermute | solution.py:21
  128.2 9.7 %collective-permute-start.6 = (bf16[1,1,64,1024]{3,2,1,0:T(8,128)(2,1)S(1)}, bf16[1,1,64,1024]{3,2,1,0:T(8,128)(2,1)S(1)}, u32[]{:S(2)}, u32[]{:S(2)}) collective-permute-start(bf16[1,1,64,1024]{3,2,1,0:T(8,128)(2,1)S(1)} %get-tuple-element.10), channel_id=1, source_target_pairs={{1,0},{2,1},{3,2},{4,3},{5,4},{6,5},{7,6},{9,8},{10,9},{11,10},{12... | collective-permute-start | bytes 393224 | tf_op jit(solution)/shard_map/ppermute | solution.py:22
Sparse Core Ops, SparseCore 0:
  120.8 365.1 all-gather.3
